TPU v7x, 512 devices: a whole 4x8x8 slice. The times are simulated.
512 devices in a mesh: dp: 256 (over z, y, x), ctx: 2 (over core).
Axes of the slice: x: 4, y: 8, z: 8, core: 2. Of those that a mesh axis runs over, the one named last changes fastest.
Arguments:
- head_inputs: bfloat16 [256, 512, 1024], P('dp', 'ctx'), may hold values from -6 to 6
- cotangent: bfloat16 [256, 512, 1024], P('dp', 'ctx'), may hold values from -6 to 6
- write_proj: bfloat16 [256, 512, 256], P('dp', 'ctx'), may hold values from -3 to 3
- read_proj: bfloat16 [256, 512, 256], P('dp', 'ctx'), may hold values from -3 to 3
- step_raw: float32 [256, 512, 16], P('dp', 'ctx'), may hold values from -4 to 4
- doc_index: int32 [256, 512], P('dp', 'ctx'), may hold values from 0 to 15, never falling along the last dimension, each value on 1 to 257 neighbouring positions
- log_rate: float32 [16], replicated, may hold values from 0 to 2.77
- step_bias: float32 [16], replicated, may hold values from -6.9 to -2.25
- skip_gain: float32 [16], replicated, may hold values from 0.5 to 1.5
Outputs:
- grad_inputs: bfloat16 [256, 512, 1024], P('dp', 'ctx')
- grad_write: bfloat16 [256, 512, 256], P('dp', 'ctx')
- grad_read: bfloat16 [256, 512, 256], P('dp', 'ctx')
- grad_step: float32 [256, 512, 16], P('dp', 'ctx')
- grad_rate: float32 [16], replicated
- grad_bias: float32 [16], replicated
- grad_skip: float32 [16], replicated
Inputs may be any that keep to these rules, and one draw needn't show every extreme that they name: doc_index never falls along a sequence; each document spans 1 to 257 tokens and one of each sequence spans exactly that many.
All inputs are finite; a program needn't handle non-finite values.
Results may differ from a plain program's by a relative error of at most 0.0025.
Values may be sent and summed in bfloat16 or wider, within the bound.
No kernel may reach another device: no remote copies, remote signals or barrier semaphores. Data moves between devices by JAX's collectives and lax.ppermute only.
A program may use at most 64 MiB of HBM per device.

v0:
```python
import jax
import jax.numpy as jnp
from jax import lax
from jax.sharding import PartitionSpec as P

HEADS = 16
HEAD_DIM = 64
STATE = 256
BLOCK = 256


def ssd_forward(
    inputs, writes, reads, steps, segment, segment_prev, state_init, log_rate, skip_gain
):
    length, heads, width = inputs.shape
    count = length // BLOCK
    rate_all = steps * (-jnp.exp(log_rate))[None, :]
    blocks = (
        inputs.reshape(count, BLOCK, heads, width),
        writes.reshape(count, BLOCK, -1),
        reads.reshape(count, BLOCK, -1),
        steps.reshape(count, BLOCK, heads),
        rate_all.reshape(count, BLOCK, heads),
        segment.reshape(count, BLOCK),
    )
    causal = jnp.arange(BLOCK)[:, None] >= jnp.arange(BLOCK)[None, :]
    highest = lax.Precision.HIGHEST

    def advance(carry, piece):
        state, last_doc = carry
        in_block, write_block, read_block, step_block, rate_block, doc_block = piece
        cumulative = jnp.cumsum(rate_block, axis=0)
        same_doc = causal & (doc_block[:, None] == doc_block[None, :])
        gaps = cumulative[:, None, :] - cumulative[None, :, :]
        decay = jnp.exp(jnp.where(same_doc[:, :, None], gaps, -1e30))
        scores = jnp.einsum("in,jn->ij", read_block, write_block, precision=highest)
        mixing = decay * (scores[:, :, None] * step_block[None, :, :])
        result = jnp.einsum("ijh,jhp->ihp", mixing, in_block, precision=highest)
        keep = (doc_block == last_doc).astype(jnp.float32)
        start = jnp.exp(cumulative) * keep[:, None]
        result = (
            result
            + jnp.einsum("in,hpn->ihp", read_block, state, precision=highest) * start[:, :, None]
        )
        result = result + skip_gain[None, :, None] * in_block
        end_doc = doc_block[BLOCK - 1]
        tail = (
            jnp.exp(cumulative[BLOCK - 1][None, :] - cumulative)
            * (doc_block == end_doc).astype(jnp.float32)[:, None]
            * step_block
        )
        carried = jnp.exp(cumulative[BLOCK - 1]) * (end_doc == last_doc).astype(jnp.float32)
        state = carried[:, None, None] * state + jnp.einsum(
            "jh,jhp,jn->hpn", tail, in_block, write_block, precision=highest
        )
        return ((state, end_doc), result)

    (state, _), results = lax.scan(jax.checkpoint(advance), (state_init, segment_prev), blocks)
    return (results.reshape(length, heads, width), state)


def layer_grads(
    inputs,
    cotangent,
    writes,
    reads,
    step_raw,
    segment,
    segment_prev,
    state_init,
    log_rate,
    step_bias,
    skip_gain,
    state_grad,
):
    length = inputs.shape[0]
    heads = step_raw.shape[1]
    head_view = inputs.astype(jnp.float32).reshape(length, heads, HEAD_DIM)

    def forward(head_view, writes, reads, step_raw, log_rate, step_bias, skip_gain):
        steps = jax.nn.softplus(step_raw + step_bias[None, :])
        return ssd_forward(
            head_view, writes, reads, steps, segment, segment_prev, state_init, log_rate, skip_gain
        )

    _, pullback = jax.vjp(
        forward,
        head_view,
        writes.astype(jnp.float32),
        reads.astype(jnp.float32),
        step_raw,
        log_rate,
        step_bias,
        skip_gain,
    )
    return pullback((cotangent.astype(jnp.float32).reshape(length, heads, HEAD_DIM), state_grad))


def on_device(
    head_inputs,
    cotangent,
    write_proj,
    read_proj,
    step_raw,
    doc_index,
    log_rate,
    step_bias,
    skip_gain,
):
    group_size = lax.axis_size("ctx")
    per_device = HEADS // group_size
    first_head = lax.axis_index("ctx") * per_device
    head_rows, cotan_rows = (
        lax.all_to_all(head_inputs, "ctx", split_axis=2, concat_axis=1, tiled=True),
        lax.all_to_all(cotangent, "ctx", split_axis=2, concat_axis=1, tiled=True),
    )
    raw_steps = lax.all_to_all(step_raw, "ctx", split_axis=2, concat_axis=1, tiled=True)
    write_all, read_all = (
        lax.all_gather(write_proj, "ctx", axis=1, tiled=True),
        lax.all_gather(read_proj, "ctx", axis=1, tiled=True),
    )
    segment = lax.all_gather(doc_index, "ctx", axis=1, tiled=True)[0]
    length = segment.shape[0]
    rate_here = lax.dynamic_slice_in_dim(log_rate, first_head, per_device)
    bias_here = lax.dynamic_slice_in_dim(step_bias, first_head, per_device)
    skip_here = lax.dynamic_slice_in_dim(skip_gain, first_head, per_device)
    zero_state = jnp.zeros((per_device, HEAD_DIM, STATE), jnp.float32)
    grads = layer_grads(
        head_rows[0],
        cotan_rows[0],
        write_all[0],
        read_all[0],
        raw_steps[0],
        segment,
        segment[0],
        zero_state,
        rate_here,
        bias_here,
        skip_here,
        zero_state,
    )
    out_inputs = lax.all_to_all(
        grads[0].reshape(1, length, per_device * HEAD_DIM).astype(jnp.bfloat16),
        "ctx",
        split_axis=1,
        concat_axis=2,
        tiled=True,
    )
    out_step = lax.all_to_all(grads[3][None], "ctx", split_axis=1, concat_axis=2, tiled=True)
    sum_write, sum_read = (
        lax.psum_scatter(grads[1][None], "ctx", scatter_dimension=1, tiled=True),
        lax.psum_scatter(grads[2][None], "ctx", scatter_dimension=1, tiled=True),
    )
    out_write = sum_write.astype(jnp.bfloat16)
    out_read = sum_read.astype(jnp.bfloat16)

    def place(values):
        return lax.dynamic_update_slice_in_dim(
            jnp.zeros((HEADS,), jnp.float32), values, first_head, 0
        )

    partial_sums = (place(grads[4]), place(grads[5]), place(grads[6]))
    total_rate, total_bias, total_skip = lax.psum(
        (partial_sums[0], partial_sums[1], partial_sums[2]), ("dp", "ctx")
    )
    return (out_inputs, out_write, out_read, out_step, total_rate, total_bias, total_skip)


def solution(mesh):
    placed = (
        P("dp", "ctx", None),
        P("dp", "ctx", None),
        P("dp", "ctx", None),
        P("dp", "ctx", None),
        P("dp", "ctx", None),
        P("dp", "ctx"),
        P(),
        P(),
        P(),
    )
    return jax.shard_map(
        on_device,
        mesh=mesh,
        in_specs=placed,
        out_specs=(
            P("dp", "ctx", None),
            P("dp", "ctx", None),
            P("dp", "ctx", None),
            P("dp", "ctx", None),
            P(),
            P(),
            P(),
        ),
        check_vma=False,
    )
```

profile of v0, /device:TPU:1, one launch (start us, length us, event | category | flops | bytes accessed | tf_op | source)
XLA Modules:
  0.0 267.5 jit_solution(3828304413454677464)
XLA Ops:
  7.2 2.4 copy.57
  10.2 3.9 %reduce.18 = bf16[1024,256]{1,0:T(8,128)(2,1)S(1)} reduce(bf16[1024,1,256]{2,1,0:T(2,128)(2,1)S(1)} %bitcast.276, bf16[]{:T(256)} %broadcast.266), dimensions={1}, to_apply=%bitcast.160.reduce_sub_computation | reduce | bytes 1048578
  15.0 10.5 %all-to-all-start.1 = ((bf16[2,2,65536]{2,1,0:T(2,128)(2,1)}), bf16[2,2,65536]{2,1,0:T(2,128)(2,1)S(1)}, u32[]{:S(2)}, u32[]{:S(2)}) async-start(bf16[2,2,65536]{2,1,0:T(2,128)(2,1)} %reshape.420), calls=%async_computation.1 | async-start | bytes 1048576 | tf_op jit(solution)/shard_map/all_to_all | solution.py:114
  30.4 2.0 all_gather.10
  32.4 2.0 all_gather.11
  34.4 2.4 copy.58
  36.8 4.7 %reduce.19 = bf16[1024,256]{1,0:T(8,128)(2,1)} reduce(bf16[1024,1,256]{2,1,0:T(2,128)(2,1)S(1)} %bitcast.280, bf16[]{:T(256)} %broadcast.266), dimensions={1}, to_apply=%bitcast.162.reduce_sub_computation | reduce | bytes 1048578
  41.5 1.8 reshape.422
  43.3 4.4 %all-to-all-start.2 = ((bf16[2,2,65536]{2,1,0:T(2,128)(2,1)}), bf16[2,2,65536]{2,1,0:T(2,128)(2,1)}, u32[]{:S(2)}, u32[]{:S(2)}) async-start(bf16[2,2,65536]{2,1,0:T(2,128)(2,1)} %reshape.422), calls=%async_computation.2 | async-start | bytes 1048576 | tf_op jit(solution)/shard_map/all_to_all | solution.py:115
  50.4 3.3 %all-to-all-start = ((f32[1,256,16]{1,0,2:T(1,128)}), f32[1,256,16]{1,0,2:T(1,128)S(1)}, u32[]{:S(2)}, u32[]{:S(2)}) async-start(f32[1,256,16]{1,0,2:T(1,128)} %copy.56), calls=%async_computation | async-start | bytes 32768 | tf_op jit(solution)/shard_map/all_to_all | solution.py:117
  58.1 13.2 %while.44 = (s32[]{:T(128)}, f32[8,64,256]{2,1,0:T(8,128)S(1)}, s32[]{:T(128)}, f32[2,8,64,256]{3,2,1,0:T(8,128)}, s32[2]{0:T(128)S(1)}, /*index=5*/f32[2,256,8]...) while((s32[]{:T(128)}, f32[8,64,256]{2,1,0:T(8,128)S(1)}, ...), condition=%wide.region_3.4_spmd.clone, body=%wide.region_0.3_spmd.clone.sunk | while | flops 403577376 | bytes 2971505 | solution.py:58
  62.8 1.9 convolution_add_fusion.6
  69.4 1.9 convolution_add_fusion.6
  75.0 60.5 %while.45 = (s32[]{:T(128)}, f32[8]{0:T(128)}, f32[8,64,256]{2,1,0:T(8,128)}, bf16[2,256,8,64]{1,3,2,0:T(8,128)(2,1)}, f32[2,256,256]{2,1,0:T(8,128)}, /*index=5...) while((s32[]{:T(128)}, f32[8]{0:T(128)}, ...), condition=%wide.region_17.18_spmd.clone, body=%wide.region_4.0_spmd.clone.sunk | while | flops 3434652672 | bytes 35708892 | solution.py:58
  86.1 4.1 %fusion.109 = (f32[256,8]{0,1:T(8,128)}, f32[256,8]{0,1:T(8,128)}, f32[256,8]{0,1:T(8,128)}, f32[256,256]{1,0:T(8,128)S(1)}) fusion(f32[256,8]{0,1:T(8,128)S(1)} %get-tuple-element.914, f32[256,256]{1,0:T(8,128)S(1)} %fusion.108, f32[256,8]{0,1:T(8,128)S(1)} %get-tuple-element.912, pred[256,256]{1,0:T(8,128)(4,1)S(1)} %compare_and_fusion.2, ...), kind=kOutput, calls=%fused_computation.30.clone.1 | convolution fusion | flops 409397248 | bytes 1679360 | tf_op jit(solution)/shard_map/transpose(jvp())/while/body/eval_jaxpr/checkpoint/ijh,jhp->ihp/dot_general | solution.py:38
  94.8 3.6 %fusion.112 = bf16[2,256,8,64]{1,3,2,0:T(8,128)(2,1)} fusion(bf16[2,256,8,64]{1,3,2,0:T(8,128)(2,1)} %get-tuple-element.993, s32[]{:T(128)S(6)} %sub.194, f32[256,8]{0,1:T(8,128)S(1)} %get-tuple-element.914, f32[256,256]{1,0:T(8,128)} %copy-done.1, f32[256,8]{0,1:T(8,128)S(1)} %get-tuple-element.912, pred[256,256]{1,0:T(8,128)(4,1)S(1)} %compare_and_fusion.2, ...), kind=kOutput, calls=%fused_computation.33.clone.1 | convolution fusion | flops 405274624 | bytes 2458116 | tf_op jit(solution)/shard_map/transpose(jvp())/while/body/eval_jaxpr/checkpoint/ijh,jhp->ihp/dot_general | solution.py:38
  101.4 2.5 reduce-window.70
  116.9 4.0 %fusion.109 = (f32[256,8]{0,1:T(8,128)}, f32[256,8]{0,1:T(8,128)}, f32[256,8]{0,1:T(8,128)}, f32[256,256]{1,0:T(8,128)S(1)}) fusion(f32[256,8]{0,1:T(8,128)S(1)} %get-tuple-element.914, f32[256,256]{1,0:T(8,128)S(1)} %fusion.108, f32[256,8]{0,1:T(8,128)S(1)} %get-tuple-element.912, pred[256,256]{1,0:T(8,128)(4,1)S(1)} %compare_and_fusion.2, ...), kind=kOutput, calls=%fused_computation.30.clone.1 | convolution fusion | flops 409397248 | bytes 1679360 | tf_op jit(solution)/shard_map/transpose(jvp())/while/body/eval_jaxpr/checkpoint/ijh,jhp->ihp/dot_general | solution.py:38
  125.5 3.6 %fusion.112 = bf16[2,256,8,64]{1,3,2,0:T(8,128)(2,1)} fusion(bf16[2,256,8,64]{1,3,2,0:T(8,128)(2,1)} %get-tuple-element.993, s32[]{:T(128)S(6)} %sub.194, f32[256,8]{0,1:T(8,128)S(1)} %get-tuple-element.914, f32[256,256]{1,0:T(8,128)} %copy-done.1, f32[256,8]{0,1:T(8,128)S(1)} %get-tuple-element.912, pred[256,256]{1,0:T(8,128)(4,1)S(1)} %compare_and_fusion.2, ...), kind=kOutput, calls=%fused_computation.33.clone.1 | convolution fusion | flops 405274624 | bytes 2458116 | tf_op jit(solution)/shard_map/transpose(jvp())/while/body/eval_jaxpr/checkpoint/ijh,jhp->ihp/dot_general | solution.py:38
  132.2 2.5 reduce-window.70
  140.1 3.3 %all-to-all-start.4 = ((f32[2,1,2048]{2,1,0:T(1,128)}), f32[2,1,2048]{2,1,0:T(1,128)S(1)}, u32[]{:S(2)}, u32[]{:S(2)}) async-start(f32[2,1,2048]{2,1,0:T(1,128)} %reshape.426), calls=%async_computation.6 | async-start | bytes 32768 | tf_op jit(solution)/shard_map/all_to_all | solution.py:149
  143.4 99.9 %all-reduce.2 = (f32[16]{0:T(128)}, f32[16]{0:T(128)}, f32[16]{0:T(128)}) all-reduce(f32[16]{0:T(128)S(1)} %multiply_dynamic-update-slice_fusion, f32[16]{0:T(128)S(1)} %dynamic_update_slice.66, f32[16]{0:T(128)S(1)} %dynamic_update_slice.67), channel_id=1, replica_groups=mesh['dp'=256,'ctx'=2] {'dp','ctx'}, use_global_device_ids=true, to_apply=%region_21.22 | all-reduce | flops 48 | bytes 384 | tf_op jit(solution)/shard_map/psum | solution.py:163
  244.6 3.9 %reduce.20 = bf16[512,512]{1,0:T(8,128)(2,1)S(1)} reduce(bf16[512,1,512]{2,1,0:T(2,128)(2,1)S(1)} %bitcast.277, bf16[]{:T(256)} %broadcast.266), dimensions={1}, to_apply=%bitcast.164.reduce_sub_computation | reduce | bytes 1048578
  249.5 4.2 %all-to-all-start.3 = ((bf16[2,2,65536]{2,1,0:T(2,128)(2,1)}), bf16[2,2,65536]{2,1,0:T(2,128)(2,1)S(1)}, u32[]{:S(2)}, u32[]{:S(2)}) async-start(bf16[2,2,65536]{2,1,0:T(2,128)(2,1)} %reshape.424), calls=%async_computation.3 | async-start | bytes 1048576 | tf_op jit(solution)/shard_map/all_to_all | solution.py:142
  (276 shorter events, 74.8 us)
Async XLA Ops:
  14.0 11.4 %copy-start.32 = (f32[16]{0:T(128)S(1)}, f32[16]{0:T(128)}, u32[]{:S(2)}) copy-start(f32[16]{0:T(128)} %param.20) | copy-start | bytes 196
  14.1 11.5 %copy-start.30 = (f32[16]{0:T(128)S(1)}, f32[16]{0:T(128)}, u32[]{:S(2)}) copy-start(f32[16]{0:T(128)} %param.19) | copy-start | bytes 196
  14.1 11.6 %copy-start.33 = (f32[16]{0:T(128)S(1)}, f32[16]{0:T(128)}, u32[]{:S(2)}) copy-start(f32[16]{0:T(128)} %param.21) | copy-start | bytes 196
  14.1 12.2 %copy-start.29 = (s32[1,256]{1,0:T(1,128)S(1)}, s32[1,256]{1,0:T(1,128)}, u32[]{:S(2)}) copy-start(s32[1,256]{1,0:T(1,128)} %param.18) | copy-start | bytes 3076
  14.1 15.6 %copy-start.20 = (f32[1,256,16]{1,2,0:T(8,128)S(1)}, f32[1,256,16]{1,2,0:T(8,128)}, u32[]{:S(2)}) copy-start(f32[1,256,16]{1,2,0:T(8,128)} %param.17) | copy-start | bytes 49156
  14.1 16.3 %copy-start.16 = (bf16[1,256,256]{2,1,0:T(8,128)(2,1)S(1)}, bf16[1,256,256]{2,1,0:T(8,128)(2,1)}, u32[]{:S(2)}) copy-start(bf16[1,256,256]{2,1,0:T(8,128)(2,1)} %param.15) | copy-start | bytes 393220
  15.0 17.4 %copy-start.17 = (bf16[1,256,256]{2,1,0:T(8,128)(2,1)S(1)}, bf16[1,256,256]{2,1,0:T(8,128)(2,1)}, u32[]{:S(2)}) copy-start(bf16[1,256,256]{2,1,0:T(8,128)(2,1)} %param.16) | copy-start | bytes 393220
  15.0 28.3 %all-to-all-start.1 = ((bf16[2,2,65536]{2,1,0:T(2,128)(2,1)}), bf16[2,2,65536]{2,1,0:T(2,128)(2,1)S(1)}, u32[]{:S(2)}, u32[]{:S(2)}) async-start(bf16[2,2,65536]{2,1,0:T(2,128)(2,1)} %reshape.420), calls=%async_computation.1 | async-start | bytes 1048576 | tf_op jit(solution)/shard_map/all_to_all | solution.py:114
  25.6 31.9 %copy-start.25 = (f32[8]{0:T(128)}, f32[8]{0:T(128)S(1)}, u32[]{:S(2)}) copy-start(f32[8]{0:T(128)S(1)} %dynamic_slice.111) | copy-start | bytes 100
  25.6 31.8 %copy-start.27 = (f32[8]{0:T(128)}, f32[8]{0:T(128)S(1)}, u32[]{:S(2)}) copy-start(f32[8]{0:T(128)S(1)} %fusion.50) | copy-start | bytes 100
  43.3 7.0 %all-to-all-start.2 = ((bf16[2,2,65536]{2,1,0:T(2,128)(2,1)}), bf16[2,2,65536]{2,1,0:T(2,128)(2,1)}, u32[]{:S(2)}, u32[]{:S(2)}) async-start(bf16[2,2,65536]{2,1,0:T(2,128)(2,1)} %reshape.422), calls=%async_computation.2 | async-start | bytes 1048576 | tf_op jit(solution)/shard_map/all_to_all | solution.py:115
  50.4 7.1 %all-to-all-start = ((f32[1,256,16]{1,0,2:T(1,128)}), f32[1,256,16]{1,0,2:T(1,128)S(1)}, u32[]{:S(2)}, u32[]{:S(2)}) async-start(f32[1,256,16]{1,0,2:T(1,128)} %copy.56), calls=%async_computation | async-start | bytes 32768 | tf_op jit(solution)/shard_map/all_to_all | solution.py:117
  53.6 203.8 %reduce-scatter.3.cloned.1.call-start = ((), (), s32[]{:S(2)}) async-start(), calls=%async_computation.7 | async-start | bytes 786432 | tf_op jit(solution)/shard_map/reduce_scatter | solution.py:151
  82.4 9.5 %copy-start.7 = (f32[256]{0:T(256)}, f32[256]{0:T(256)S(1)}, u32[]{:S(2)}) copy-start(f32[256]{0:T(256)S(1)} %get-tuple-element.920) | copy-start | bytes 3076 | tf_op jit(solution)/shard_map/transpose(jvp())/while
  83.5 8.5 %copy-start.11 = (f32[8]{0:T(128)}, f32[8]{0:T(128)S(1)}, u32[]{:S(2)}) copy-start(f32[8]{0:T(128)S(1)} %get-tuple-element.913) | copy-start | bytes 100 | tf_op jit(solution)/shard_map/transpose(jvp())/while
  99.4 5.3 %copy-start.19 = (s32[2,256]{1,0:T(2,128)S(1)}, s32[2,256]{1,0:T(2,128)}, u32[]{:S(2)}) copy-start(s32[2,256]{1,0:T(2,128)} %copy-done.18) | copy-start | bytes 6148 | tf_op jit(solution)/shard_map/transpose(jvp())/while
  99.4 5.3 %copy-start.35 = (s32[2]{0:T(128)S(1)}, s32[2]{0:T(128)}, u32[]{:S(2)}) copy-start(s32[2]{0:T(128)} %copy-done.34) | copy-start | bytes 28 | tf_op jit(solution)/shard_map/transpose(jvp())/while
  113.2 9.5 %copy-start.7 = (f32[256]{0:T(256)}, f32[256]{0:T(256)S(1)}, u32[]{:S(2)}) copy-start(f32[256]{0:T(256)S(1)} %get-tuple-element.920) | copy-start | bytes 3076 | tf_op jit(solution)/shard_map/transpose(jvp())/while
  114.3 8.4 %copy-start.11 = (f32[8]{0:T(128)}, f32[8]{0:T(128)S(1)}, u32[]{:S(2)}) copy-start(f32[8]{0:T(128)S(1)} %get-tuple-element.913) | copy-start | bytes 100 | tf_op jit(solution)/shard_map/transpose(jvp())/while
  130.1 5.3 %copy-start.19 = (s32[2,256]{1,0:T(2,128)S(1)}, s32[2,256]{1,0:T(2,128)}, u32[]{:S(2)}) copy-start(s32[2,256]{1,0:T(2,128)} %copy-done.18) | copy-start | bytes 6148 | tf_op jit(solution)/shard_map/transpose(jvp())/while
  135.6 107.7 %copy-start.4 = (bf16[2,256,8,64]{1,3,2,0:T(8,128)(2,1)S(1)}, bf16[2,256,8,64]{1,3,2,0:T(8,128)(2,1)}, u32[]{:S(2)}) copy-start(bf16[2,256,8,64]{1,3,2,0:T(8,128)(2,1)} %get-tuple-element.448) | copy-start | bytes 1572868
  135.6 123.4 %reduce-scatter.5.cloned.1.call-start = ((), (), s32[]{:S(2)}) async-start(), calls=%async_computation.8 | async-start | bytes 786432 | tf_op jit(solution)/shard_map/reduce_scatter | solution.py:152
  140.1 109.4 %all-to-all-start.4 = ((f32[2,1,2048]{2,1,0:T(1,128)}), f32[2,1,2048]{2,1,0:T(1,128)S(1)}, u32[]{:S(2)}, u32[]{:S(2)}) async-start(f32[2,1,2048]{2,1,0:T(1,128)} %reshape.426), calls=%async_computation.6 | async-start | bytes 32768 | tf_op jit(solution)/shard_map/all_to_all | solution.py:149
  249.5 6.0 %all-to-all-start.3 = ((bf16[2,2,65536]{2,1,0:T(2,128)(2,1)}), bf16[2,2,65536]{2,1,0:T(2,128)(2,1)S(1)}, u32[]{:S(2)}, u32[]{:S(2)}) async-start(bf16[2,2,65536]{2,1,0:T(2,128)(2,1)} %reshape.424), calls=%async_computation.3 | async-start | bytes 1048576 | tf_op jit(solution)/shard_map/all_to_all | solution.py:142
  (37 other events, 78.1 us)
Sparse Core Ops, SparseCore 0:
  135.7 16.2 reduce-scatter.2
  155.1 17.3 reduce-scatter.4
where the time goes:
time: 269 us; the launch traced here: 267 us
  blocking collectives  106 us (39%)
  other arithmetic  44.1 us (16%)
  local copies, waits for them, and re-layouts  38.4 us (14%)
  matrix products  32.5 us (12%)
  starting transfers between devices  26 us (10%)
  between operations  14.4 us (5%)
  loops' own time  5.8 us (2%)
    psum x1, blocking collectives, on_device(): lax.psum((partial_sums[0], partial_sums[1], partial_sums[2]), ('dp', 'ctx'))  99.9 us
    unnamed x54, local copies, waits for them, and re-layouts  17.9 us
    dot_general x4, matrix products, advance(): result = jnp.einsum('ijh,jhp->ihp', mixing, in_block, precision=highest)  15.2 us
    unnamed x7, other arithmetic  13.7 us
    all_to_all x1, starting transfers between devices, on_device(): lax.all_to_all(head_inputs, 'ctx', split_axis=2, concat_axis=1, tiled=True)  10.5 us
    another operation x17, other arithmetic  9.32 us
    dot_general x6, matrix products, advance(): jnp.einsum('jh,jhp,jn->hpn', tail, in_block, write_block, precision=highest)  7.06 us
    dot_general x6, matrix products, advance(): jnp.einsum('in,hpn->ihp', read_block, state, precision=highest)  6.04 us
  transfers between devices with their start and end apart: 7, of which 0 were waited for; matrix products, arithmetic and copies ran while one was open for 12% of the time, Pallas kernels for 0%

commit v1 on v0

--- a/solution.py
+++ b/solution.py
@@ -111,7 +111,12 @@
     per_device = HEADS // group_size
     first_head = lax.axis_index("ctx") * per_device
     head_rows, cotan_rows = (
-        lax.all_to_all(head_inputs, "ctx", split_axis=2, concat_axis=1, tiled=True),
+        jnp.concatenate(
+            lax.all_to_all(
+                jnp.stack(jnp.split(head_inputs, lax.axis_size("ctx"), axis=2)), "ctx", 0, 0
+            ),
+            axis=1,
+        ),
         lax.all_to_all(cotangent, "ctx", split_axis=2, concat_axis=1, tiled=True),
     )
     raw_steps = lax.all_to_all(step_raw, "ctx", split_axis=2, concat_axis=1, tiled=True)

time: 269 us -> 259 us (0.963)
  other arithmetic: 44.1 us -> 39.2 us
  local copies, waits for them, and re-layouts: 38.4 us -> 34 us
    unnamed x54 -> x52, local copies, waits for them, and re-layouts: 17.9 us -> 11.1 us
    all_to_all x1, starting transfers between devices: 4.39 us -> 10.5 us  [on_device(): lax.all_to_all(cotangent, 'ctx', split_axis=2, concat_axis=1, tiled=True)]
    all_to_all x1, starting transfers between devices: 10.5 us -> 4.4 us  [on_device(): lax.all_to_all(jnp.stack(jnp.split(head_inputs, lax.axis_size('ctx'), axi...]
    unnamed x7 -> x6, other arithmetic: 13.7 us -> 9.02 us
    another operation x17 -> x18, other arithmetic: 9.32 us -> 10.2 us
  transfers between devices with their start and end apart: 7 -> 7, of which waited for: 0 -> 0; matrix products, arithmetic and copies ran while one was open for 12% -> 9% of each run, Pallas kernels for 0% -> 0%
where the time goes in v1:
time: 259 us; the launch traced here: 258 us
  blocking collectives  106 us (41%)
  other arithmetic  39.2 us (15%)
  local copies, waits for them, and re-layouts  34 us (13%)
  matrix products  32.5 us (13%)
  starting transfers between devices  25.9 us (10%)
  between operations  14.4 us (6%)
  loops' own time  5.8 us (2%)
    psum x1, blocking collectives, on_device(): lax.psum((partial_sums[0], partial_sums[1], partial_sums[2]), ('dp', 'ctx'))  99.9 us
    dot_general x4, matrix products, advance(): result = jnp.einsum('ijh,jhp->ihp', mixing, in_block, precision=highest)  15.2 us
    unnamed x52, local copies, waits for them, and re-layouts  11.1 us
    all_to_all x1, starting transfers between devices, on_device(): lax.all_to_all(cotangent, 'ctx', split_axis=2, concat_axis=1, tiled=True)  10.5 us
    another operation x17, other arithmetic  9.32 us
    unnamed x6, other arithmetic  9.02 us
    dot_general x6, matrix products, advance(): jnp.einsum('jh,jhp,jn->hpn', tail, in_block, write_block, precision=highest)  7.05 us
    dot_general x6, matrix products, advance(): jnp.einsum('in,hpn->ihp', read_block, state, precision=highest)  6.03 us
  transfers between devices with their start and end apart: 7, of which 0 were waited for; matrix products, arithmetic and copies ran while one was open for 9% of the time, Pallas kernels for 0%

profile of v1, /device:TPU:1, one launch (start us, length us, event | category | flops | bytes accessed | tf_op | source)
XLA Modules:
  0.0 258.0 jit_solution(15500171456586835572)
XLA Ops:
  7.2 2.4 copy.58
  10.2 3.9 %reduce.18 = bf16[1024,256]{1,0:T(8,128)(2,1)S(1)} reduce(bf16[1024,1,256]{2,1,0:T(2,128)(2,1)S(1)} %bitcast.274, bf16[]{:T(256)} %broadcast.266), dimensions={1}, to_apply=%bitcast.160.reduce_sub_computation | reduce | bytes 1048578
  15.0 10.5 %all-to-all-start.2 = ((bf16[2,2,65536]{2,1,0:T(2,128)(2,1)}), bf16[2,2,65536]{2,1,0:T(2,128)(2,1)S(1)}, u32[]{:S(2)}, u32[]{:S(2)}) async-start(bf16[2,2,65536]{2,1,0:T(2,128)(2,1)} %reshape.416), calls=%async_computation.2 | async-start | bytes 1048576 | tf_op jit(solution)/shard_map/all_to_all | solution.py:120
  26.2 1.8 all_gather.9
  30.4 2.0 all_gather.10
  32.4 2.1 all_gather.11
  35.5 4.4 %all-to-all-start.1 = ((bf16[2,1,256,512]{3,2,1,0:T(8,128)(2,1)}), bf16[2,1,256,512]{3,2,1,0:T(8,128)(2,1)}, u32[]{:S(2)}, u32[]{:S(2)}) async-start(bf16[2,1,256,512]{3,2,1,0:T(8,128)(2,1)} %pad_maximum_fusion), calls=%async_computation.1 | async-start | bytes 1048576 | tf_op jit(solution)/shard_map/all_to_all | solution.py:115
  42.5 3.3 %all-to-all-start = ((f32[1,256,16]{1,0,2:T(1,128)}), f32[1,256,16]{1,0,2:T(1,128)S(1)}, u32[]{:S(2)}, u32[]{:S(2)}) async-start(f32[1,256,16]{1,0,2:T(1,128)} %copy.56), calls=%async_computation | async-start | bytes 32768 | tf_op jit(solution)/shard_map/all_to_all | solution.py:122
  45.8 2.3 copy.57
  48.7 13.2 %while.44 = (s32[]{:T(128)}, f32[8,64,256]{2,1,0:T(8,128)S(1)}, s32[]{:T(128)}, f32[2,8,64,256]{3,2,1,0:T(8,128)}, s32[2]{0:T(128)S(1)}, /*index=5*/f32[2,256,8]...) while((s32[]{:T(128)}, f32[8,64,256]{2,1,0:T(8,128)S(1)}, ...), condition=%wide.region_3.4_spmd.clone, body=%wide.region_0.3_spmd.clone.sunk | while | flops 403577376 | bytes 2971505 | solution.py:58
  53.4 1.9 convolution_add_fusion.6
  60.0 1.9 convolution_add_fusion.6
  65.6 60.4 %while.45 = (s32[]{:T(128)}, f32[8]{0:T(128)}, f32[8,64,256]{2,1,0:T(8,128)}, bf16[2,256,8,64]{1,3,2,0:T(8,128)(2,1)}, f32[2,256,256]{2,1,0:T(8,128)}, /*index=5...) while((s32[]{:T(128)}, f32[8]{0:T(128)}, ...), condition=%wide.region_17.18_spmd.clone, body=%wide.region_4.0_spmd.clone.sunk | while | flops 3434652672 | bytes 35708892 | solution.py:58
  76.7 4.0 %fusion.109 = (f32[256,8]{0,1:T(8,128)}, f32[256,8]{0,1:T(8,128)}, f32[256,8]{0,1:T(8,128)}, f32[256,256]{1,0:T(8,128)S(1)}) fusion(f32[256,8]{0,1:T(8,128)S(1)} %get-tuple-element.916, f32[256,256]{1,0:T(8,128)S(1)} %fusion.108, f32[256,8]{0,1:T(8,128)S(1)} %get-tuple-element.914, pred[256,256]{1,0:T(8,128)(4,1)S(1)} %compare_and_fusion.2, ...), kind=kOutput, calls=%fused_computation.30.clone.1 | convolution fusion | flops 409397248 | bytes 1679360 | tf_op jit(solution)/shard_map/transpose(jvp())/while/body/eval_jaxpr/checkpoint/ijh,jhp->ihp/dot_general | solution.py:38
  85.3 3.6 %fusion.112 = bf16[2,256,8,64]{1,3,2,0:T(8,128)(2,1)} fusion(bf16[2,256,8,64]{1,3,2,0:T(8,128)(2,1)} %get-tuple-element.995, s32[]{:T(128)S(6)} %sub.194, f32[256,8]{0,1:T(8,128)S(1)} %get-tuple-element.916, f32[256,256]{1,0:T(8,128)} %copy-done.1, f32[256,8]{0,1:T(8,128)S(1)} %get-tuple-element.914, pred[256,256]{1,0:T(8,128)(4,1)S(1)} %compare_and_fusion.2, ...), kind=kOutput, calls=%fused_computation.33.clone.1 | convolution fusion | flops 405274624 | bytes 2458116 | tf_op jit(solution)/shard_map/transpose(jvp())/while/body/eval_jaxpr/checkpoint/ijh,jhp->ihp/dot_general | solution.py:38
  92.0 2.5 reduce-window.70
  107.5 4.0 %fusion.109 = (f32[256,8]{0,1:T(8,128)}, f32[256,8]{0,1:T(8,128)}, f32[256,8]{0,1:T(8,128)}, f32[256,256]{1,0:T(8,128)S(1)}) fusion(f32[256,8]{0,1:T(8,128)S(1)} %get-tuple-element.916, f32[256,256]{1,0:T(8,128)S(1)} %fusion.108, f32[256,8]{0,1:T(8,128)S(1)} %get-tuple-element.914, pred[256,256]{1,0:T(8,128)(4,1)S(1)} %compare_and_fusion.2, ...), kind=kOutput, calls=%fused_computation.30.clone.1 | convolution fusion | flops 409397248 | bytes 1679360 | tf_op jit(solution)/shard_map/transpose(jvp())/while/body/eval_jaxpr/checkpoint/ijh,jhp->ihp/dot_general | solution.py:38
  116.1 3.6 %fusion.112 = bf16[2,256,8,64]{1,3,2,0:T(8,128)(2,1)} fusion(bf16[2,256,8,64]{1,3,2,0:T(8,128)(2,1)} %get-tuple-element.995, s32[]{:T(128)S(6)} %sub.194, f32[256,8]{0,1:T(8,128)S(1)} %get-tuple-element.916, f32[256,256]{1,0:T(8,128)} %copy-done.1, f32[256,8]{0,1:T(8,128)S(1)} %get-tuple-element.914, pred[256,256]{1,0:T(8,128)(4,1)S(1)} %compare_and_fusion.2, ...), kind=kOutput, calls=%fused_computation.33.clone.1 | convolution fusion | flops 405274624 | bytes 2458116 | tf_op jit(solution)/shard_map/transpose(jvp())/while/body/eval_jaxpr/checkpoint/ijh,jhp->ihp/dot_general | solution.py:38
  122.7 2.5 reduce-window.70
  130.7 3.3 %all-to-all-start.4 = ((f32[2,1,2048]{2,1,0:T(1,128)}), f32[2,1,2048]{2,1,0:T(1,128)S(1)}, u32[]{:S(2)}, u32[]{:S(2)}) async-start(f32[2,1,2048]{2,1,0:T(1,128)} %reshape.420), calls=%async_computation.6 | async-start | bytes 32768 | tf_op jit(solution)/shard_map/all_to_all | solution.py:154
  134.0 99.9 %all-reduce.2 = (f32[16]{0:T(128)}, f32[16]{0:T(128)}, f32[16]{0:T(128)}) all-reduce(f32[16]{0:T(128)S(1)} %multiply_dynamic-update-slice_fusion, f32[16]{0:T(128)S(1)} %dynamic_update_slice.66, f32[16]{0:T(128)S(1)} %dynamic_update_slice.67), channel_id=1, replica_groups=mesh['dp'=256,'ctx'=2] {'dp','ctx'}, use_global_device_ids=true, to_apply=%region_21.22 | all-reduce | flops 48 | bytes 384 | tf_op jit(solution)/shard_map/psum | solution.py:168
  235.1 3.9 %reduce.19 = bf16[512,512]{1,0:T(8,128)(2,1)S(1)} reduce(bf16[512,1,512]{2,1,0:T(2,128)(2,1)S(1)} %bitcast.275, bf16[]{:T(256)} %broadcast.266), dimensions={1}, to_apply=%bitcast.162.reduce_sub_computation | reduce | bytes 1048578
  240.1 4.2 %all-to-all-start.3 = ((bf16[2,2,65536]{2,1,0:T(2,128)(2,1)}), bf16[2,2,65536]{2,1,0:T(2,128)(2,1)S(1)}, u32[]{:S(2)}, u32[]{:S(2)}) async-start(bf16[2,2,65536]{2,1,0:T(2,128)(2,1)} %reshape.418), calls=%async_computation.3 | async-start | bytes 1048576 | tf_op jit(solution)/shard_map/all_to_all | solution.py:147
  248.0 1.6 convert_element_type.106
  (275 shorter events, 68.4 us)
Async XLA Ops:
  14.0 11.4 %copy-start.33 = (f32[16]{0:T(128)S(1)}, f32[16]{0:T(128)}, u32[]{:S(2)}) copy-start(f32[16]{0:T(128)} %param.20) | copy-start | bytes 196
  14.1 11.5 %copy-start.31 = (f32[16]{0:T(128)S(1)}, f32[16]{0:T(128)}, u32[]{:S(2)}) copy-start(f32[16]{0:T(128)} %param.19) | copy-start | bytes 196
  14.1 11.6 %copy-start.34 = (f32[16]{0:T(128)S(1)}, f32[16]{0:T(128)}, u32[]{:S(2)}) copy-start(f32[16]{0:T(128)} %param.21) | copy-start | bytes 196
  14.1 12.2 %copy-start.30 = (s32[1,256]{1,0:T(1,128)S(1)}, s32[1,256]{1,0:T(1,128)}, u32[]{:S(2)}) copy-start(s32[1,256]{1,0:T(1,128)} %param.18) | copy-start | bytes 3076
  14.1 15.6 %copy-start.21 = (f32[1,256,16]{1,2,0:T(8,128)S(1)}, f32[1,256,16]{1,2,0:T(8,128)}, u32[]{:S(2)}) copy-start(f32[1,256,16]{1,2,0:T(8,128)} %param.17) | copy-start | bytes 49156
  14.1 16.3 %copy-start.17 = (bf16[1,256,256]{2,1,0:T(8,128)(2,1)S(1)}, bf16[1,256,256]{2,1,0:T(8,128)(2,1)}, u32[]{:S(2)}) copy-start(bf16[1,256,256]{2,1,0:T(8,128)(2,1)} %param.15) | copy-start | bytes 393220
  15.0 17.4 %copy-start.18 = (bf16[1,256,256]{2,1,0:T(8,128)(2,1)S(1)}, bf16[1,256,256]{2,1,0:T(8,128)(2,1)}, u32[]{:S(2)}) copy-start(bf16[1,256,256]{2,1,0:T(8,128)(2,1)} %param.16) | copy-start | bytes 393220
  15.0 20.5 %all-to-all-start.2 = ((bf16[2,2,65536]{2,1,0:T(2,128)(2,1)}), bf16[2,2,65536]{2,1,0:T(2,128)(2,1)S(1)}, u32[]{:S(2)}, u32[]{:S(2)}) async-start(bf16[2,2,65536]{2,1,0:T(2,128)(2,1)} %reshape.416), calls=%async_computation.2 | async-start | bytes 1048576 | tf_op jit(solution)/shard_map/all_to_all | solution.py:120
  25.6 22.5 %copy-start.26 = (f32[8]{0:T(128)}, f32[8]{0:T(128)S(1)}, u32[]{:S(2)}) copy-start(f32[8]{0:T(128)S(1)} %dynamic_slice.111) | copy-start | bytes 100
  25.6 22.4 %copy-start.28 = (f32[8]{0:T(128)}, f32[8]{0:T(128)S(1)}, u32[]{:S(2)}) copy-start(f32[8]{0:T(128)S(1)} %fusion.50) | copy-start | bytes 100
  35.5 7.0 %all-to-all-start.1 = ((bf16[2,1,256,512]{3,2,1,0:T(8,128)(2,1)}), bf16[2,1,256,512]{3,2,1,0:T(8,128)(2,1)}, u32[]{:S(2)}, u32[]{:S(2)}) async-start(bf16[2,1,256,512]{3,2,1,0:T(8,128)(2,1)} %pad_maximum_fusion), calls=%async_computation.1 | async-start | bytes 1048576 | tf_op jit(solution)/shard_map/all_to_all | solution.py:115
  42.5 5.6 %all-to-all-start = ((f32[1,256,16]{1,0,2:T(1,128)}), f32[1,256,16]{1,0,2:T(1,128)S(1)}, u32[]{:S(2)}, u32[]{:S(2)}) async-start(f32[1,256,16]{1,0,2:T(1,128)} %copy.56), calls=%async_computation | async-start | bytes 32768 | tf_op jit(solution)/shard_map/all_to_all | solution.py:122
  45.8 202.2 %reduce-scatter.3.cloned.1.call-start = ((), (), s32[]{:S(2)}) async-start(), calls=%async_computation.7 | async-start | bytes 786432 | tf_op jit(solution)/shard_map/reduce_scatter | solution.py:156
  73.0 9.5 %copy-start.8 = (f32[256]{0:T(256)}, f32[256]{0:T(256)S(1)}, u32[]{:S(2)}) copy-start(f32[256]{0:T(256)S(1)} %get-tuple-element.922) | copy-start | bytes 3076 | tf_op jit(solution)/shard_map/transpose(jvp())/while
  74.1 8.5 %copy-start.12 = (f32[8]{0:T(128)}, f32[8]{0:T(128)S(1)}, u32[]{:S(2)}) copy-start(f32[8]{0:T(128)S(1)} %get-tuple-element.915) | copy-start | bytes 100 | tf_op jit(solution)/shard_map/transpose(jvp())/while
  90.0 5.3 %copy-start.20 = (s32[2,256]{1,0:T(2,128)S(1)}, s32[2,256]{1,0:T(2,128)}, u32[]{:S(2)}) copy-start(s32[2,256]{1,0:T(2,128)} %copy-done.19) | copy-start | bytes 6148 | tf_op jit(solution)/shard_map/transpose(jvp())/while
  90.0 5.3 %copy-start.36 = (s32[2]{0:T(128)S(1)}, s32[2]{0:T(128)}, u32[]{:S(2)}) copy-start(s32[2]{0:T(128)} %copy-done.35) | copy-start | bytes 28 | tf_op jit(solution)/shard_map/transpose(jvp())/while
  103.8 9.5 %copy-start.8 = (f32[256]{0:T(256)}, f32[256]{0:T(256)S(1)}, u32[]{:S(2)}) copy-start(f32[256]{0:T(256)S(1)} %get-tuple-element.922) | copy-start | bytes 3076 | tf_op jit(solution)/shard_map/transpose(jvp())/while
  104.8 8.4 %copy-start.12 = (f32[8]{0:T(128)}, f32[8]{0:T(128)S(1)}, u32[]{:S(2)}) copy-start(f32[8]{0:T(128)S(1)} %get-tuple-element.915) | copy-start | bytes 100 | tf_op jit(solution)/shard_map/transpose(jvp())/while
  120.7 5.3 %copy-start.20 = (s32[2,256]{1,0:T(2,128)S(1)}, s32[2,256]{1,0:T(2,128)}, u32[]{:S(2)}) copy-start(s32[2,256]{1,0:T(2,128)} %copy-done.19) | copy-start | bytes 6148 | tf_op jit(solution)/shard_map/transpose(jvp())/while
  126.1 107.7 %copy-start.4 = (bf16[2,256,8,64]{1,3,2,0:T(8,128)(2,1)S(1)}, bf16[2,256,8,64]{1,3,2,0:T(8,128)(2,1)}, u32[]{:S(2)}) copy-start(bf16[2,256,8,64]{1,3,2,0:T(8,128)(2,1)} %get-tuple-element.448) | copy-start | bytes 1572868
  126.2 123.4 %reduce-scatter.5.cloned.1.call-start = ((), (), s32[]{:S(2)}) async-start(), calls=%async_computation.8 | async-start | bytes 786432 | tf_op jit(solution)/shard_map/reduce_scatter | solution.py:157
  130.7 109.4 %all-to-all-start.4 = ((f32[2,1,2048]{2,1,0:T(1,128)}), f32[2,1,2048]{2,1,0:T(1,128)S(1)}, u32[]{:S(2)}, u32[]{:S(2)}) async-start(f32[2,1,2048]{2,1,0:T(1,128)} %reshape.420), calls=%async_computation.6 | async-start | bytes 32768 | tf_op jit(solution)/shard_map/all_to_all | solution.py:154
  240.1 6.0 %all-to-all-start.3 = ((bf16[2,2,65536]{2,1,0:T(2,128)(2,1)}), bf16[2,2,65536]{2,1,0:T(2,128)(2,1)S(1)}, u32[]{:S(2)}, u32[]{:S(2)}) async-start(bf16[2,2,65536]{2,1,0:T(2,128)(2,1)} %reshape.418), calls=%async_computation.3 | async-start | bytes 1048576 | tf_op jit(solution)/shard_map/all_to_all | solution.py:147
  (38 other events, 80.3 us)
Sparse Core Ops, SparseCore 0:
  126.3 16.2 reduce-scatter.2
  145.6 17.3 reduce-scatter.4
